TPU v7x, 32 devices: a whole 2x2x4 slice. The times are simulated.
32 devices in a mesh: shard: 2 (over x), ctx: 4 (over z), tensor: 4 (over y, core).
Axes of the slice: x: 2, y: 2, z: 4, core: 2. Of those that a mesh axis runs over, the one named last changes fastest.
Arguments:
- inputs: bfloat16 [1024, 8, 1024], P('ctx', 'shard'), may hold values from -6 to 6
- time_features: bfloat16 [8, 256], P('shard'), may hold values from -1 to 1
- valid_mask: int32 [1024, 8], P('ctx', 'shard'), may hold values from 0 to 1, as said below
- teacher: bfloat16 [1024, 8, 1024], P('ctx', 'shard'), may hold values from -6 to 6
- w_time: bfloat16 [256, 1024], replicated, may hold values from -0.375 to 0.375
- b_time: float32 [1024], replicated, may hold values from -2 to 2
- w_query: bfloat16 [1024, 1024], P('shard', 'tensor'), may hold values from -0.1875 to 0.1875
- b_query: float32 [1024], P('tensor'), may hold values from -2 to 2
- w_key: bfloat16 [1024, 1024], P('shard', 'tensor'), may hold values from -0.1875 to 0.1875
- w_value: bfloat16 [1024, 1024], P('shard', 'tensor'), may hold values from -0.1875 to 0.1875
- b_value: float32 [1024], P('tensor'), may hold values from -0.3 to 0.3
- w_output: bfloat16 [1024, 1024], P('shard', 'tensor'), may hold values from -1.5 to 1.5
- b_output: float32 [1024], replicated, may hold values from -2 to 2
- gain_one: float32 [1024], replicated, may hold values from 0.5 to 1.5
- shift_one: float32 [1024], replicated, may hold values from -2 to 2
- w_hidden: bfloat16 [1024, 4096], P('shard', 'tensor'), may hold values from -0.1875 to 0.1875
- b_hidden: float32 [4096], P('tensor'), may hold values from -2 to 2
- w_down: bfloat16 [1024, 4096], P('shard', 'tensor'), may hold values from -0.09375 to 0.09375
- b_down: float32 [1024], replicated, may hold values from -2 to 2
- gain_two: float32 [1024], replicated, may hold values from 0.5 to 1.5
- shift_two: float32 [1024], replicated, may hold values from -2 to 2
Outputs:
- layer_out: bfloat16 [1024, 8, 1024], P('ctx', 'shard')
- loss: float32 [], replicated
- grad_inputs: float32 [1024, 8, 1024], P('ctx', 'shard')
- grad_w_time: float32 [256, 1024], replicated
- grad_b_time: float32 [1024], replicated
- grad_w_query: float32 [1024, 1024], P(('shard', 'ctx'), 'tensor')
- grad_b_query: float32 [1024], P('tensor')
- grad_w_key: float32 [1024, 1024], P(('shard', 'ctx'), 'tensor')
- grad_w_value: float32 [1024, 1024], P(('shard', 'ctx'), 'tensor')
- grad_b_value: float32 [1024], P('tensor')
- grad_w_output: float32 [1024, 1024], P(('shard', 'ctx'), 'tensor')
- grad_b_output: float32 [1024], replicated
- grad_gain_one: float32 [1024], replicated
- grad_shift_one: float32 [1024], replicated
- grad_w_hidden: float32 [1024, 4096], P(('shard', 'ctx'), 'tensor')
- grad_b_hidden: float32 [4096], P('tensor')
- grad_w_down: float32 [1024, 4096], P(('shard', 'ctx'), 'tensor')
- grad_b_down: float32 [1024], replicated
- grad_gain_two: float32 [1024], replicated
- grad_shift_two: float32 [1024], replicated
Inputs may be any that keep to these rules, and one draw needn't show every extreme that they name: `valid_mask`: 0 or 1; the last token of every sequence is valid.
All inputs are finite; a program needn't handle non-finite values.
Results may differ from a plain program's by a relative error of at most 0.018.
Values may be sent and summed in bfloat16 or wider, within the bound.
No kernel may reach another device: no remote copies, remote signals or barrier semaphores. Data moves between devices by JAX's collectives and lax.ppermute only.
A program may use at most 256 MiB of HBM per device.

v0:
```python
from functools import partial
import math
import jax
import jax.numpy as jnp
from jax import lax
from jax.sharding import PartitionSpec as P

D = 1024
HEADS = 16


def layer_norm(value, gain, shift):
    center = jnp.mean(value, axis=-1, keepdims=True)
    offset = value - center
    spread = jnp.mean(offset * offset, axis=-1, keepdims=True)
    return offset * lax.rsqrt(spread + 1e-05) * gain + shift


def contract(left, right, left_dim, right_dim):
    return lax.dot_general(
        left, right, (((left_dim,), (right_dim,)), ((), ())), preferred_element_type=jnp.float32
    )


def block_rows(length):
    return math.gcd(length, 512)


def score_block(queries, keys, scale):
    return jnp.einsum("qshd,kshd->qshk", queries, keys, preferred_element_type=jnp.float32) * scale


def fold_block(carry, keys, values, queries, scale):
    peak, total, summed = carry
    scores = score_block(queries, keys, scale)
    new_peak = jnp.maximum(peak, jnp.max(scores, axis=-1))
    fade = jnp.exp(peak - new_peak)
    weights = jnp.exp(scores - new_peak[..., None])
    total = total * fade + jnp.sum(weights, axis=-1)
    summed = summed * fade[..., None] + jnp.einsum(
        "qshk,kshd->qshd", weights.astype(jnp.bfloat16), values, preferred_element_type=jnp.float32
    )
    return (new_peak, total, summed)


def fold_keys(carry, piece, start, queries, scale):
    keys, values = piece
    length, seqs, width = keys.shape
    heads = queries.shape[2]
    head_size = width // heads
    block = block_rows(length)
    blocks = length // block
    keys = keys.reshape(blocks, block, seqs, heads, head_size)
    values = values.reshape(blocks, block, seqs, heads, head_size)

    def step(inner, pair):
        return (fold_block(inner, pair[0], pair[1], queries, scale), None)

    carry, unused = lax.scan(step, carry, (keys, values))
    return carry


def score_grads(keys, values, queries, out_grad, logsum, delta, scale):
    scores = score_block(queries, keys, scale)
    weights = jnp.exp(scores - logsum[..., None])
    weight_grad = jnp.einsum(
        "qshd,kshd->qshk", out_grad, values, preferred_element_type=jnp.float32
    )
    score_grad = (weights * (weight_grad - delta[..., None])).astype(jnp.bfloat16)
    return (weights, score_grad)


def pair_grads(keys, values, queries, out_grad, logsum, delta, scale):
    block, seqs = (keys.shape[0], keys.shape[1])
    weights, score_grad = score_grads(keys, values, queries, out_grad, logsum, delta, scale)
    value_grad = jnp.einsum(
        "qshk,qshd->kshd",
        weights.astype(jnp.bfloat16),
        out_grad,
        preferred_element_type=jnp.float32,
    )
    key_grad = (
        jnp.einsum("qshk,qshd->kshd", score_grad, queries, preferred_element_type=jnp.float32)
        * scale
    )
    joined = jnp.concatenate(
        [key_grad.reshape(block, seqs, -1), value_grad.reshape(block, seqs, -1)], axis=-1
    )
    return (score_grad, joined)


def back_block(query_grad, pair, queries, out_grad, logsum, delta, scale):
    keys, values = pair
    score_grad, joined = pair_grads(keys, values, queries, out_grad, logsum, delta, scale)
    query_grad = (
        query_grad
        + jnp.einsum("qshk,kshd->qshd", score_grad, keys, preferred_element_type=jnp.float32)
        * scale
    )
    return (query_grad, joined)


def body(
    inputs,
    time_features,
    valid_mask,
    teacher,
    w_time,
    b_time,
    w_query,
    b_query,
    w_key,
    w_value,
    b_value,
    w_output,
    b_output,
    gain_one,
    shift_one,
    w_hidden,
    b_hidden,
    w_down,
    b_down,
    gain_two,
    shift_two,
):
    positions, seqs, width = inputs.shape
    rows_local = positions * seqs
    head_size = D // HEADS
    scale = 1.0 / math.sqrt(head_size)
    embed = jnp.dot(time_features, w_time, preferred_element_type=jnp.float32) + b_time
    start = (inputs.astype(jnp.float32) + embed[None]).reshape(rows_local, width)
    start_low = start.astype(jnp.bfloat16)
    full_query, full_key, full_value, full_output = (
        lax.all_gather(w_query, "shard", axis=0, tiled=True),
        lax.all_gather(w_key, "shard", axis=0, tiled=True),
        lax.all_gather(w_value, "shard", axis=0, tiled=True),
        lax.all_gather(w_output, "shard", axis=0, tiled=True),
    )
    columns = full_query.shape[1]
    heads = columns // head_size
    query_low = (
        jnp.dot(start_low, full_query, preferred_element_type=jnp.float32) + b_query
    ).astype(jnp.bfloat16)
    key_low = jnp.dot(start_low, full_key, preferred_element_type=jnp.float32).astype(jnp.bfloat16)
    value_low = (
        jnp.dot(start_low, full_value, preferred_element_type=jnp.float32) + b_value
    ).astype(jnp.bfloat16)
    queries = query_low.reshape(positions, seqs, heads, head_size)
    key_local = key_low.reshape(positions, seqs, columns)
    value_local = value_low.reshape(positions, seqs, columns)
    initial = (
        jnp.full((positions, seqs, heads), -1e30, jnp.float32),
        jnp.zeros((positions, seqs, heads), jnp.float32),
        jnp.zeros((positions, seqs, heads, head_size), jnp.float32),
    )
    folder = partial(fold_keys, queries=queries, scale=scale)
    peak, total, summed = folder(
        initial,
        (
            lax.all_gather(key_local, "ctx", axis=0, tiled=True),
            lax.all_gather(value_local, "ctx", axis=0, tiled=True),
        ),
        jnp.int32(0),
    )
    attended = summed / total[..., None]
    logsum = peak + jnp.log(total)
    mixed_low = attended.reshape(rows_local, columns).astype(jnp.bfloat16)
    branch_part = contract(mixed_low, full_output, 1, 1)
    branch = lax.psum(branch_part.astype(jnp.bfloat16), "tensor").astype(jnp.float32) + b_output
    normed, norm_back_one = jax.vjp(layer_norm, start + branch, gain_one, shift_one)
    normed_low = normed.astype(jnp.bfloat16)
    full_hidden, full_down = (
        lax.all_gather(w_hidden, "shard", axis=0, tiled=True),
        lax.all_gather(w_down, "shard", axis=0, tiled=True),
    )
    pre_act = jnp.dot(normed_low, full_hidden, preferred_element_type=jnp.float32) + b_hidden
    hidden, gelu_back = jax.vjp(partial(jax.nn.gelu, approximate=False), pre_act)
    hidden_low = hidden.astype(jnp.bfloat16)
    feed_part = contract(hidden_low, full_down, 1, 1)
    feed = lax.psum(feed_part.astype(jnp.bfloat16), "tensor").astype(jnp.float32) + b_down
    result, norm_back_two = jax.vjp(layer_norm, normed + feed, gain_two, shift_two)
    layer_out = result.astype(jnp.bfloat16).reshape(positions, seqs, width)
    valid = valid_mask.astype(jnp.float32).reshape(rows_local)
    error = result - teacher.reshape(rows_local, width).astype(jnp.float32)
    squares_local = jnp.sum(valid[:, None] * error * error)
    squares_total, count = lax.psum((squares_local, jnp.sum(valid)), ("shard", "ctx"))
    loss = squares_total / (D * count)
    tokens_all = rows_local * lax.axis_size("ctx") * lax.axis_size("shard")
    result_grad = 2.0 * tokens_all / count * valid[:, None] * error
    sum_grad, grad_gain_two, grad_shift_two = norm_back_two(result_grad)
    feed_low = sum_grad.astype(jnp.bfloat16)
    grad_down = contract(feed_low, hidden_low, 0, 0)
    hidden_grad = jnp.dot(feed_low, full_down, preferred_element_type=jnp.float32)
    pre_grad = gelu_back(hidden_grad)[0].astype(jnp.bfloat16)
    grad_hidden = contract(normed_low, pre_grad, 0, 0)
    normed_part = contract(pre_grad, full_hidden, 1, 1)
    normed_grad = sum_grad + lax.psum(normed_part.astype(jnp.bfloat16), "tensor").astype(
        jnp.float32
    )
    first_grad, grad_gain_one, grad_shift_one = norm_back_one(normed_grad)
    branch_low = first_grad.astype(jnp.bfloat16)
    grad_output = contract(branch_low, mixed_low, 0, 0)
    mixed_grad = jnp.dot(branch_low, full_output, preferred_element_type=jnp.float32).astype(
        jnp.bfloat16
    )
    out_grad = mixed_grad.reshape(positions, seqs, heads, head_size)
    delta = jnp.sum(out_grad.astype(jnp.float32) * attended, axis=-1)
    all_keys, all_values = (
        lax.all_gather(key_local, "ctx", axis=0, tiled=True),
        lax.all_gather(value_local, "ctx", axis=0, tiled=True),
    )
    length = all_keys.shape[0]
    block = block_rows(length)
    key_blocks = all_keys.reshape(length // block, block, seqs, heads, head_size)
    value_blocks = all_values.reshape(length // block, block, seqs, heads, head_size)
    query_zero = jnp.zeros((positions, seqs, heads, head_size), jnp.float32)
    back_step = partial(
        back_block, queries=queries, out_grad=out_grad, logsum=logsum, delta=delta, scale=scale
    )
    query_grad, joined = lax.scan(back_step, query_zero, (key_blocks, value_blocks))
    joined = joined.reshape(length, seqs, 2 * columns)
    owned = lax.psum_scatter(
        joined.astype(jnp.bfloat16), "ctx", scatter_dimension=0, tiled=True
    ).astype(jnp.float32)
    key_grad_low = owned[:, :, :columns].reshape(rows_local, columns).astype(jnp.bfloat16)
    value_grad_low = owned[:, :, columns:].reshape(rows_local, columns).astype(jnp.bfloat16)
    query_grad_low = query_grad.reshape(rows_local, columns).astype(jnp.bfloat16)
    grad_query = contract(start_low, query_grad_low, 0, 0)
    grad_key = contract(start_low, key_grad_low, 0, 0)
    grad_value = contract(start_low, value_grad_low, 0, 0)
    start_part = (
        contract(query_grad_low, full_query, 1, 1)
        + contract(key_grad_low, full_key, 1, 1)
        + contract(value_grad_low, full_value, 1, 1)
    )
    start_grad = first_grad + lax.psum(start_part.astype(jnp.bfloat16), "tensor").astype(
        jnp.float32
    )
    grad_inputs = start_grad.reshape(positions, seqs, width)
    embed_grad = jnp.sum(grad_inputs, axis=0)
    time_grad = jnp.dot(
        time_features.astype(jnp.float32).T, embed_grad, precision=lax.Precision.HIGHEST
    )
    (
        grad_w_time,
        grad_b_time,
        grad_b_query,
        grad_b_value,
        grad_b_output,
        grad_gain_one,
        grad_shift_one,
        grad_b_hidden,
        grad_b_down,
        grad_gain_two,
        grad_shift_two,
    ) = lax.psum(
        (
            time_grad,
            jnp.sum(embed_grad, axis=0),
            jnp.sum(query_grad_low.astype(jnp.float32), axis=0),
            jnp.sum(value_grad_low.astype(jnp.float32), axis=0),
            jnp.sum(branch_low.astype(jnp.float32), axis=0),
            grad_gain_one,
            grad_shift_one,
            jnp.sum(pre_grad.astype(jnp.float32), axis=0),
            jnp.sum(feed_low.astype(jnp.float32), axis=0),
            grad_gain_two,
            grad_shift_two,
        ),
        ("shard", "ctx"),
    )
    grad_w_query, grad_w_key, grad_w_value, grad_w_output, grad_w_hidden, grad_w_down = (
        lax.psum_scatter(grad_query, ("shard", "ctx"), scatter_dimension=0, tiled=True),
        lax.psum_scatter(grad_key, ("shard", "ctx"), scatter_dimension=0, tiled=True),
        lax.psum_scatter(grad_value, ("shard", "ctx"), scatter_dimension=0, tiled=True),
        lax.psum_scatter(grad_output, ("shard", "ctx"), scatter_dimension=0, tiled=True),
        lax.psum_scatter(grad_hidden, ("shard", "ctx"), scatter_dimension=0, tiled=True),
        lax.psum_scatter(grad_down, ("shard", "ctx"), scatter_dimension=0, tiled=True),
    )
    return (
        layer_out,
        loss,
        grad_inputs,
        grad_w_time,
        grad_b_time,
        grad_w_query,
        grad_b_query,
        grad_w_key,
        grad_w_value,
        grad_b_value,
        grad_w_output,
        grad_b_output,
        grad_gain_one,
        grad_shift_one,
        grad_w_hidden,
        grad_b_hidden,
        grad_w_down,
        grad_b_down,
        grad_gain_two,
        grad_shift_two,
    )


def solution(mesh):
    placed = (
        P("ctx", "shard", None),
        P("shard", None),
        P("ctx", "shard"),
        P("ctx", "shard", None),
        P(),
        P(),
        P("shard", "tensor"),
        P("tensor"),
        P("shard", "tensor"),
        P("shard", "tensor"),
        P("tensor"),
        P("shard", "tensor"),
        P(),
        P(),
        P(),
        P("shard", "tensor"),
        P("tensor"),
        P("shard", "tensor"),
        P(),
        P(),
        P(),
    )
    return jax.shard_map(
        body,
        mesh=mesh,
        in_specs=placed,
        out_specs=(
            P("ctx", "shard", None),
            P(),
            P("ctx", "shard", None),
            P(),
            P(),
            P(("shard", "ctx"), "tensor"),
            P("tensor"),
            P(("shard", "ctx"), "tensor"),
            P(("shard", "ctx"), "tensor"),
            P("tensor"),
            P(("shard", "ctx"), "tensor"),
            P(),
            P(),
            P(),
            P(("shard", "ctx"), "tensor"),
            P("tensor"),
            P(("shard", "ctx"), "tensor"),
            P(),
            P(),
            P(),
        ),
        check_vma=False,
    )
```

profile of v0, /device:TPU:0, one launch (start us, length us, event | category | flops | bytes accessed | tf_op | source)
XLA Modules:
  0.0 1141.1 jit_solution(9354903953610810085)
XLA Ops:
  10.0 5.7 fusion.56
  15.6 5.3 reshape.180
  21.0 10.0 all_gather.26
  35.5 8.2 all_gather.29
  48.8 7.4 all_gather.28
  60.6 7.3 all_gather.31
  67.9 15.4 %all-gather.5.cloned.1.call-done = bf16[1024,4,256]{0,2,1:T(8,128)(2,1)} async-done(((bf16[256,4,256]{0,2,1:T(8,128)(2,1)}), bf16[1024,4,256]{0,2,1:T(8,128)(2,1)}) %all-gather.5.cloned.1.call-update) | async-done | bytes 2097168 | tf_op jit(solution)/shard_map/all_gather | solution.py:160
  83.3 4.5 reshape.182
  89.8 40.1 %all-gather.7.cloned.1.call-done = bf16[1024,4,256]{0,2,1:T(8,128)(2,1)} async-done(((bf16[256,4,256]{0,2,1:T(8,128)(2,1)}), bf16[1024,4,256]{0,2,1:T(8,128)(2,1)}) %all-gather.7.cloned.1.call-update) | async-done | bytes 2097168 | tf_op jit(solution)/shard_map/all_gather | solution.py:161
  130.0 4.5 reshape.185
  137.8 28.7 %while.28 = (s32[]{:T(128)}, f32[256,4,4]{0,2,1:T(4,128)S(1)}, f32[256,4,4]{0,2,1:T(4,128)S(1)}, f32[256,4,4,64]{0,3,2,1:T(8,128)}, bf16[2,512,4,4,64]{1,4,3,2,0...) while((s32[]{:T(128)}, f32[256,4,4]{0,2,1:T(4,128)S(1)}, ...), condition=%wide.region_3.4_spmd.clone, body=%wide.region_0.3_spmd.clone.sunk | while | flops 554455040 | bytes 63701640 | solution.py:59
  137.8 4.5 bitcast_reduce_fusion.2
  142.3 5.0 fusion.146
  148.1 3.9 fusion.148
  152.0 4.5 bitcast_reduce_fusion.2
  156.5 5.0 fusion.146
  162.3 4.2 fusion.148
  180.3 48.4 %all-reduce.7.cloned.1.call-done = bf16[1024,1024]{1,0:T(8,128)(2,1)} async-done(((bf16[1024,1024]{1,0:T(8,128)(2,1)}), bf16[1024,1024]{1,0:T(8,128)(2,1)}) %all-reduce.7.cloned.1.call-update) | async-done | bytes 2097168 | tf_op jit(solution)/shard_map/psum | solution.py:169
  234.7 15.7 %multiply_convert_fusion = (bf16[1024,1024]{1,0:T(8,128)(2,1)}, f32[1024,1024]{1,0:T(8,128)}, f32[1024,1024]{1,0:T(8,128)}) fusion(f32[1024]{0:T(1024)S(1)} %copy-done.47, bf16[1024,1024]{1,0:T(8,128)(2,1)} %all-gather.9.cloned.1.call-done, f32[1024,1024]{1,0:T(8,128)} %copy-done.4, f32[1024]{0:T(1024)S(1)} %copy-done.42, f32[1024]{0:T(1024)S(1)} %copy-done.32, ...), kind=kOutput, calls=%fused_computation.69 | convolution fusion | flops 2221932544 | bytes 16797696 | tf_op jit(solution)/shard_map/dot_general | solution.py:176
  250.4 5.9 convolution_convert_fusion.1
  257.0 22.5 %psum.122 = f32[]{:T(128)} all-reduce(f32[]{:T(128)} %convert_reduce_fusion.5), channel_id=1, replica_groups=mesh['shard'=2,'ctx'=4,'tensor'=4] {'shard','ctx'}, use_global_device_ids=true, to_apply=%region_13.14 | all-reduce | flops 1 | bytes 8 | tf_op jit(solution)/shard_map/psum | solution.py:186
  279.8 4.3 reshape.189
  284.8 23.2 %all-reduce.9.cloned.1.call-done = bf16[1024,1024]{1,0:T(8,128)(2,1)} async-done(((bf16[1024,1024]{1,0:T(8,128)(2,1)}), bf16[1024,1024]{1,0:T(8,128)(2,1)}) %all-reduce.9.cloned.1.call-update) | async-done | bytes 2097168 | tf_op jit(solution)/shard_map/psum | solution.py:180
  308.0 3.7 fusion.72
  313.9 5.5 multiply_reduce_fusion
  326.5 3.6 convert_reduce_fusion.1
  331.4 3.7 convolution_convert_fusion
  335.4 51.3 %all-reduce.11.cloned.1.call-done = bf16[1024,1024]{1,0:T(8,128)(2,1)} async-done(((bf16[1024,1024]{1,0:T(8,128)(2,1)}), bf16[1024,1024]{1,0:T(8,128)(2,1)}) %all-reduce.11.cloned.1.call-update) | async-done | bytes 2097168 | tf_op jit(solution)/shard_map/psum | solution.py:197
  386.8 5.2 multiply_reduce_fusion.1
  404.0 7.8 multiply_reduce_fusion.7
  414.7 25.0 %while.29 = (s32[]{:T(128)}, f32[256,4,4,64]{0,3,2,1:T(8,128)}, bf16[2,512,4,512]{1,3,2,0:T(8,128)(2,1)}, bf16[2,512,4,4,64]{1,4,3,2,0:T(8,128)(2,1)S(1)}, bf16[...) while((s32[]{:T(128)}, f32[256,4,4,64]{0,3,2,1:T(8,128)}, ...), condition=%wide.region_21.22_spmd.clone, body=%wide.region_20.21_spmd.clone.sunk | while | flops 1364983808 | bytes 76595896 | solution.py:220
  423.1 4.0 fusion.161
  435.5 4.3 fusion.161
  439.7 7.3 copy.94
  452.8 71.2 %reduce-scatter.8.cloned.1.call-done = bf16[256,4,512]{2,0,1:T(8,128)(2,1)} async-done(((bf16[1024,4,512]{2,0,1:T(8,128)(2,1)}), bf16[256,4,512]{2,0,1:T(8,128)(2,1)}) %reduce-scatter.8.cloned.1.call-update) | async-done | bytes 1048592 | tf_op jit(solution)/shard_map/reduce_scatter | solution.py:222
  530.0 5.5 add_convert_fusion
  535.6 52.0 %all-reduce.13.cloned.1.call-done = bf16[1024,1024]{1,0:T(8,128)(2,1)} async-done(((bf16[1024,1024]{1,0:T(8,128)(2,1)}), bf16[1024,1024]{1,0:T(8,128)(2,1)}) %all-reduce.13.cloned.1.call-update) | async-done | bytes 2097168 | tf_op jit(solution)/shard_map/psum | solution.py:236
  587.6 5.4 fusion.68
  593.0 5.2 reshape.188
  611.7 7.5 fusion.63
  619.5 6.6 fusion.80
  638.8 38.8 %all-reduce = (f32[]{:T(128)}, f32[1024]{0:T(1024)}, f32[256]{0:T(256)}, f32[256]{0:T(256)}, f32[1024]{0:T(1024)}, /*index=5*/f32[1024]{0:T(1024)}, f32[1024]{0:...) all-reduce(f32[]{:T(128)} %get-tuple-element.280, ...), channel_id=1, replica_groups=mesh['shard'=2,'ctx'=4,'tensor'=4] {'shard','ctx'}, use_global_device_ids=true, to_apply=%region_11.12 | all-reduce | flops 8705 | bytes 69640 | tf_op jit(solution)/shard_map/psum | solution.py:186
  683.5 64.4 %reduce-scatter.16.cloned.1.call-done = f32[128,256]{1,0:T(8,128)} async-done(((f32[1024,256]{1,0:T(8,128)}), f32[128,256]{1,0:T(8,128)}) %reduce-scatter.16.cloned.1.call-update) | async-done | bytes 131088 | tf_op jit(solution)/shard_map/reduce_scatter | solution.py:276
  747.9 67.0 %reduce-scatter.10.cloned.1.call-done = f32[128,256]{1,0:T(8,128)} async-done(((f32[1024,256]{1,0:T(8,128)}), f32[128,256]{1,0:T(8,128)}) %reduce-scatter.10.cloned.1.call-update) | async-done | bytes 131088 | tf_op jit(solution)/shard_map/reduce_scatter | solution.py:273
  815.0 91.1 %reduce-scatter.18.cloned.1.call-done = f32[128,1024]{1,0:T(8,128)} async-done(((f32[1024,1024]{1,0:T(8,128)}), f32[128,1024]{1,0:T(8,128)}) %reduce-scatter.18.cloned.1.call-update) | async-done | bytes 524304 | tf_op jit(solution)/shard_map/reduce_scatter | solution.py:277
  906.1 92.1 %reduce-scatter.20.cloned.1.call-done = f32[128,1024]{1,0:T(8,128)} async-done(((f32[1024,1024]{1,0:T(8,128)}), f32[128,1024]{1,0:T(8,128)}) %reduce-scatter.20.cloned.1.call-update) | async-done | bytes 524304 | tf_op jit(solution)/shard_map/reduce_scatter | solution.py:278
  998.2 67.1 %reduce-scatter.14.cloned.1.call-done = f32[128,256]{1,0:T(8,128)} async-done(((f32[1024,256]{1,0:T(8,128)}), f32[128,256]{1,0:T(8,128)}) %reduce-scatter.14.cloned.1.call-update) | async-done | bytes 131088 | tf_op jit(solution)/shard_map/reduce_scatter | solution.py:275
  1065.3 66.8 %reduce-scatter.12.cloned.1.call-done = f32[128,256]{1,0:T(8,128)} async-done(((f32[1024,256]{1,0:T(8,128)}), f32[128,256]{1,0:T(8,128)}) %reduce-scatter.12.cloned.1.call-update) | async-done | bytes 131088 | tf_op jit(solution)/shard_map/reduce_scatter | solution.py:274
  (228 shorter events, 128.5 us)
Async XLA Ops:
  8.0 75.3 %all-gather.5.cloned.1.call-start = ((), (), s32[]{:S(2)}) async-start(), calls=%async_computation.7 | async-start | bytes 2621440 | tf_op jit(solution)/shard_map/all_gather | solution.py:160
  15.6 5.3 copy-start.28
  21.0 14.5 %copy-start.29 = (bf16[512,256]{1,0:T(8,128)(2,1)S(1)}, bf16[512,256]{1,0:T(8,128)(2,1)}, u32[]{:S(2)}) copy-start(bf16[512,256]{1,0:T(8,128)(2,1)} %param.34) | copy-start | bytes 786436
  31.0 12.6 %copy-start.15 = (bf16[1024,256]{1,0:T(8,128)(2,1)}, bf16[1024,256]{1,0:T(8,128)(2,1)S(1)}, u32[]{:S(2)}) copy-start(bf16[1024,256]{1,0:T(8,128)(2,1)S(1)} %all_gather.26) | copy-start | bytes 1572868
  31.0 13.4 %copy-start.43 = (f32[256]{0:T(256)S(1)}, f32[256]{0:T(256)}, u32[]{:S(2)}) copy-start(f32[256]{0:T(256)} %param.35) | copy-start | bytes 3076
  35.4 13.4 %copy-start.30 = (bf16[512,256]{1,0:T(8,128)(2,1)S(1)}, bf16[512,256]{1,0:T(8,128)(2,1)}, u32[]{:S(2)}) copy-start(bf16[512,256]{1,0:T(8,128)(2,1)} %param.31) | copy-start | bytes 786436
  35.4 94.5 %all-gather.7.cloned.1.call-start = ((), (), s32[]{:S(2)}) async-start(), calls=%async_computation.8 | async-start | bytes 2621440 | tf_op jit(solution)/shard_map/all_gather | solution.py:161
  44.4 11.8 %copy-start.44 = (f32[256]{0:T(256)S(1)}, f32[256]{0:T(256)}, u32[]{:S(2)}) copy-start(f32[256]{0:T(256)} %param.32) | copy-start | bytes 3076
  48.7 179.9 %all-reduce.7.cloned.1.call-start = ((), (), s32[]{:S(2)}) async-start(), calls=%async_computation.9 | async-start | bytes 4194304 | tf_op jit(solution)/shard_map/psum | solution.py:169
  56.2 3.1 copy-start.19
  56.2 4.4 copy-start.31
  142.3 5.8 copy-start.2
  156.5 5.8 copy-start.2
  172.8 55.9 %copy-start.39 = (f32[1024]{0:T(1024)S(1)}, f32[1024]{0:T(1024)}, u32[]{:S(2)}) copy-start(f32[1024]{0:T(1024)} %param.37) | copy-start | bytes 12292
  178.9 55.8 %all-gather.9.cloned.1.call-start = ((), (), s32[]{:S(2)}) async-start(), calls=%async_computation.10 | async-start | bytes 3145728 | tf_op jit(solution)/shard_map/all_gather | solution.py:173
  179.4 71.0 %all-gather.11.cloned.1.call-start = ((), (), s32[]{:S(2)}) async-start(), calls=%async_computation.11 | async-start | bytes 3145728 | tf_op jit(solution)/shard_map/all_gather | solution.py:174
  180.0 128.0 %all-reduce.9.cloned.1.call-start = ((), (), s32[]{:S(2)}) async-start(), calls=%async_computation.12 | async-start | bytes 4194304 | tf_op jit(solution)/shard_map/psum | solution.py:180
  250.4 6.0 copy-start.37
  256.4 51.6 %copy-start.40 = (f32[1024]{0:T(1024)S(1)}, f32[1024]{0:T(1024)}, u32[]{:S(2)}) copy-start(f32[1024]{0:T(1024)} %param.43) | copy-start | bytes 12292
  256.4 130.4 %all-reduce.11.cloned.1.call-start = ((), (), s32[]{:S(2)}) async-start(), calls=%async_computation.13 | async-start | bytes 4194304 | tf_op jit(solution)/shard_map/psum | solution.py:197
  321.4 8.7 copy-start.7
  321.4 3.2 copy-start.46
  321.4 5.1 copy-start.49
  322.4 7.7 copy-start.23
  326.5 5.0 copy-start.45
  335.2 188.8 %reduce-scatter.8.cloned.1.call-start = ((), (), s32[]{:S(2)}) async-start(), calls=%async_computation.14 | async-start | bytes 5242880 | tf_op jit(solution)/shard_map/reduce_scatter | solution.py:222
  386.8 5.2 copy-start.5
  386.8 6.5 copy-start.8
  386.8 7.1 copy-start.14
  396.0 3.7 copy-start.26
  447.0 140.6 %all-reduce.13.cloned.1.call-start = ((), (), s32[]{:S(2)}) async-start(), calls=%async_computation.15 | async-start | bytes 4194304 | tf_op jit(solution)/shard_map/psum | solution.py:236
  450.1 75.7 %copy-start.16 = (bf16[1024,256]{1,0:T(8,128)(2,1)S(1)}, bf16[1024,256]{1,0:T(8,128)(2,1)}, u32[]{:S(2)}) copy-start(bf16[1024,256]{1,0:T(8,128)(2,1)} %copy-done.15) | copy-start | bytes 1572868
  524.0 4.4 copy-start.27
  525.7 4.2 copy-start.18
  535.5 145.5 %all-reduce.15.cloned.1.call-start = ((), (), s32[]{:S(2)}) async-start(), calls=%async_computation.16 | async-start | bytes 2097152 | tf_op jit(solution)/shard_map/psum | solution.py:256
  598.2 4.6 copy-start.25
  601.1 5.1 copy-start.11
  602.7 145.2 %reduce-scatter.16.cloned.1.call-start = ((), (), s32[]{:S(2)}) async-start(), calls=%async_computation.20 | async-start | bytes 1179648 | tf_op jit(solution)/shard_map/reduce_scatter | solution.py:276
  606.1 208.8 %reduce-scatter.10.cloned.1.call-start = ((), (), s32[]{:S(2)}) async-start(), calls=%async_computation.17 | async-start | bytes 1179648 | tf_op jit(solution)/shard_map/reduce_scatter | solution.py:273
  611.6 294.5 %reduce-scatter.18.cloned.1.call-start = ((), (), s32[]{:S(2)}) async-start(), calls=%async_computation.21 | async-start | bytes 4718592 | tf_op jit(solution)/shard_map/reduce_scatter | solution.py:277
  619.2 379.0 %reduce-scatter.20.cloned.1.call-start = ((), (), s32[]{:S(2)}) async-start(), calls=%async_computation.22 | async-start | bytes 4718592 | tf_op jit(solution)/shard_map/reduce_scatter | solution.py:278
  626.0 439.2 %reduce-scatter.14.cloned.1.call-start = ((), (), s32[]{:S(2)}) async-start(), calls=%async_computation.19 | async-start | bytes 1179648 | tf_op jit(solution)/shard_map/reduce_scatter | solution.py:275
  632.2 4.3 copy-start.13
  632.2 6.6 copy-start.34
  632.2 6.6 copy-start.35
  632.2 6.6 copy-start.36
  632.2 499.9 %reduce-scatter.12.cloned.1.call-start = ((), (), s32[]{:S(2)}) async-start(), calls=%async_computation.18 | async-start | bytes 1179648 | tf_op jit(solution)/shard_map/reduce_scatter | solution.py:274
  632.3 499.8 %copy-start.1 = (bf16[256,1024]{1,0:T(8,128)(2,1)S(1)}, bf16[256,1024]{1,0:T(8,128)(2,1)}, u32[]{:S(2)}) copy-start(bf16[256,1024]{1,0:T(8,128)(2,1)} %param.29) | copy-start | bytes 1572868
  (22 other events, 45.4 us)
Sparse Core Ops, SparseCore 0:
  35.5 47.7 all-gather.4
  85.5 44.4 all-gather.6
  179.0 49.6 all-reduce.6
  256.5 51.4 all-reduce.8
  335.3 51.4 all-reduce.10
  447.2 76.8 reduce-scatter.7
  535.7 51.9 all-reduce.12
Sparse Core Ops, SparseCore 1:
  180.9 31.2 all-gather.8
  213.7 33.0 all-gather.10
  602.8 78.2 all-reduce.14
  685.0 62.9 reduce-scatter.15
  752.3 62.6 reduce-scatter.9
  819.2 86.9 reduce-scatter.17
  910.6 87.5 reduce-scatter.19
  1002.0 63.2 reduce-scatter.13
  1069.5 62.5 reduce-scatter.11
where the time goes:
time: 1150 us; the launch traced here: 1140 us
  waiting for transfers between devices  754 us (66%)
  matrix products  123 us (11%)
  blocking collectives  94.3 us (8%)
  local copies, waits for them, and re-layouts  85 us (7%)
  other arithmetic  63.5 us (6%)
  between operations  19.9 us (2%)
    reduce_scatter x1, waiting for transfers between devices, body(): lax.psum_scatter(grad_down, ('shard', 'ctx'), scatter_dimension=0, tiled=...  92.1 us
    reduce_scatter x1, waiting for transfers between devices, body(): lax.psum_scatter(grad_hidden, ('shard', 'ctx'), scatter_dimension=0, tile...  91.1 us
    reduce_scatter x1, waiting for transfers between devices, body(): lax.psum_scatter(joined.astype(jnp.bfloat16), 'ctx', scatter_dimension=0,...  71.2 us
    reduce_scatter x1, waiting for transfers between devices, body(): lax.psum_scatter(grad_value, ('shard', 'ctx'), scatter_dimension=0, tiled...  67.1 us
    reduce_scatter x1, waiting for transfers between devices, body(): lax.psum_scatter(grad_query, ('shard', 'ctx'), scatter_dimension=0, tiled...  67 us
    reduce_scatter x1, waiting for transfers between devices, body(): lax.psum_scatter(grad_key, ('shard', 'ctx'), scatter_dimension=0, tiled=T...  66.8 us
    reduce_scatter x1, waiting for transfers between devices, body(): lax.psum_scatter(grad_output, ('shard', 'ctx'), scatter_dimension=0, tile...  64.4 us
    psum x2, blocking collectives, body(): lax.psum((squares_local, jnp.sum(valid)), ('shard', 'ctx'))  61.4 us
  transfers between devices with their start and end apart: 16, of which 14 were waited for; matrix products, arithmetic and copies ran while one was open for 7% of the time, Pallas kernels for 0%

commit v1 on v0

--- a/solution.py
+++ b/solution.py
@@ -166,7 +166,12 @@
     logsum = peak + jnp.log(total)
     mixed_low = attended.reshape(rows_local, columns).astype(jnp.bfloat16)
     branch_part = contract(mixed_low, full_output, 1, 1)
-    branch = lax.psum(branch_part.astype(jnp.bfloat16), "tensor").astype(jnp.float32) + b_output
+    branch = (
+        jnp.sum(lax.all_gather(branch_part.astype(jnp.bfloat16), "tensor"), axis=0).astype(
+            jnp.float32
+        )
+        + b_output
+    )
     normed, norm_back_one = jax.vjp(layer_norm, start + branch, gain_one, shift_one)
     normed_low = normed.astype(jnp.bfloat16)
     full_hidden, full_down = (

time: 1150 us -> 1200 us (1.043)
  waiting for transfers between devices: 754 us -> 790 us
  other arithmetic: 63.5 us -> 78.1 us
    all_gather x0 -> x1, waiting for transfers between devices: none -> 55.5 us  [body(): lax.all_gather(branch_part.astype(jnp.bfloat16), 'tensor')]
    psum x1 -> x0, waiting for transfers between devices: 48.4 us -> none  [body(): lax.psum(branch_part.astype(jnp.bfloat16), 'tensor').astype(jnp.float32)]
    all_gather x1, waiting for transfers between devices: 0.01 us -> 19 us  [body(): lax.all_gather(w_down, 'shard', axis=0, tiled=True)]
    unnamed x102 -> x105, local copies, waits for them, and re-layouts: 29.2 us -> 27.2 us
  transfers between devices with their start and end apart: 16 -> 16, of which waited for: 14 -> 16; matrix products, arithmetic and copies ran while one was open for 7% -> 9% of each run, Pallas kernels for 0% -> 0%
where the time goes in v1:
time: 1200 us; the launch traced here: 1190 us
  waiting for transfers between devices  790 us (66%)
  matrix products  122 us (10%)
  blocking collectives  93.2 us (8%)
  local copies, waits for them, and re-layouts  89 us (7%)
  other arithmetic  78.1 us (7%)
  between operations  17.9 us (1%)
    reduce_scatter x1, waiting for transfers between devices, body(): lax.psum_scatter(grad_down, ('shard', 'ctx'), scatter_dimension=0, tiled=...  91.8 us
    reduce_scatter x1, waiting for transfers between devices, body(): lax.psum_scatter(grad_hidden, ('shard', 'ctx'), scatter_dimension=0, tile...  91.6 us
    reduce_scatter x1, waiting for transfers between devices, body(): lax.psum_scatter(joined.astype(jnp.bfloat16), 'ctx', scatter_dimension=0,...  70.8 us
    reduce_scatter x1, waiting for transfers between devices, body(): lax.psum_scatter(grad_value, ('shard', 'ctx'), scatter_dimension=0, tiled...  67.3 us
    reduce_scatter x1, waiting for transfers between devices, body(): lax.psum_scatter(grad_key, ('shard', 'ctx'), scatter_dimension=0, tiled=T...  66.4 us
    reduce_scatter x1, waiting for transfers between devices, body(): lax.psum_scatter(grad_output, ('shard', 'ctx'), scatter_dimension=0, tile...  66.4 us
    reduce_scatter x1, waiting for transfers between devices, body(): lax.psum_scatter(grad_query, ('shard', 'ctx'), scatter_dimension=0, tiled...  64.8 us
    psum x2, blocking collectives, body(): lax.psum((squares_local, jnp.sum(valid)), ('shard', 'ctx'))  60.1 us
  transfers between devices with their start and end apart: 16, of which 16 were waited for; matrix products, arithmetic and copies ran while one was open for 9% of the time, Pallas kernels for 0%

profile of v1, /device:TPU:0, one launch (start us, length us, event | category | flops | bytes accessed | tf_op | source)
XLA Modules:
  0.0 1191.6 jit_solution(6065568280686438069)
XLA Ops:
  9.1 4.2 convert_add_fusion.2
  13.3 5.3 reshape.211
  18.7 10.0 all_gather.32
  33.2 8.2 all_gather.35
  46.5 7.4 all_gather.34
  58.3 7.4 all_gather.37
  65.8 15.2 %all-gather.7.cloned.1.call-done = bf16[1024,4,256]{0,2,1:T(8,128)(2,1)} async-done(((bf16[256,4,256]{0,2,1:T(8,128)(2,1)}), bf16[1024,4,256]{0,2,1:T(8,128)(2,1)}) %all-gather.7.cloned.1.call-update) | async-done | bytes 2097168 | tf_op jit(solution)/shard_map/all_gather | solution.py:160
  81.0 4.5 reshape.213
  87.5 40.1 %all-gather.9.cloned.1.call-done = bf16[1024,4,256]{0,2,1:T(8,128)(2,1)} async-done(((bf16[256,4,256]{0,2,1:T(8,128)(2,1)}), bf16[1024,4,256]{0,2,1:T(8,128)(2,1)}) %all-gather.9.cloned.1.call-update) | async-done | bytes 2097168 | tf_op jit(solution)/shard_map/all_gather | solution.py:161
  127.7 4.5 reshape.216
  135.5 28.7 %while.28 = (s32[]{:T(128)}, f32[256,4,4]{0,2,1:T(4,128)S(1)}, f32[256,4,4]{0,2,1:T(4,128)S(1)}, f32[256,4,4,64]{0,3,2,1:T(8,128)}, bf16[2,512,4,4,64]{1,4,3,2,0...) while((s32[]{:T(128)}, f32[256,4,4]{0,2,1:T(4,128)S(1)}, ...), condition=%wide.region_3.4_spmd.clone, body=%wide.region_0.3_spmd.clone.sunk | while | flops 554455040 | bytes 63701640 | solution.py:59
  135.5 4.5 bitcast_reduce_fusion.2
  140.1 5.0 fusion.145
  149.7 4.5 bitcast_reduce_fusion.2
  154.2 5.0 fusion.145
  177.8 55.5 %all-gather.15.cloned.1.call-done = bf16[4096,1024]{1,0:T(8,128)(2,1)} async-done(((bf16[1024,1024]{1,0:T(8,128)(2,1)}), bf16[4096,1024]{1,0:T(8,128)(2,1)}) %all-gather.15.cloned.1.call-update) | async-done | bytes 8388624 | tf_op jit(solution)/shard_map/all_gather | solution.py:170
  233.2 7.4 reduce_sum.219
  240.6 5.4 reshape.220
  246.0 5.0 fusion.57
  251.2 4.5 multiply_reduce_fusion.5
  258.6 9.2 all-gather.11.cloned.1.call-done
  267.8 15.5 %multiply_convert_fusion = (bf16[1024,1024]{1,0:T(8,128)(2,1)}, f32[1024,1024]{1,0:T(8,128)}, f32[1024,1024]{1,0:T(8,128)}) fusion(f32[1024]{0:T(1024)S(1)} %copy-done.48, bf16[1024,1024]{1,0:T(8,128)(2,1)} %all-gather.11.cloned.1.call-done, f32[1024,1024]{1,0:T(8,128)} %add_subtract_fusion, f32[1024]{0:T(1024)S(1)} %copy-done.43, f32[1024]{0:T(1024)S(1)} %copy-done.33, ...), kind=kOutput, calls=%fused_computation.69 | convolution fusion | flops 2220883968 | bytes 16793600 | tf_op jit(solution)/shard_map/dot_general | solution.py:181
  283.3 19.0 %all-gather.13.cloned.1.call-done = bf16[1024,1024]{1,0:T(8,128)(2,1)} async-done(((bf16[512,1024]{1,0:T(8,128)(2,1)}), bf16[1024,1024]{1,0:T(8,128)(2,1)}) %all-gather.13.cloned.1.call-update) | async-done | bytes 2097168 | tf_op jit(solution)/shard_map/all_gather | solution.py:179
  302.3 5.9 convolution_convert_fusion.1
  308.9 21.3 %psum.114 = f32[]{:T(128)} all-reduce(f32[]{:T(128)} %convert_reduce_fusion.5), channel_id=1, replica_groups=mesh['shard'=2,'ctx'=4,'tensor'=4] {'shard','ctx'}, use_global_device_ids=true, to_apply=%region_13.14 | all-reduce | flops 1 | bytes 8 | tf_op jit(solution)/shard_map/psum | solution.py:191
  330.5 4.3 reshape.221
  335.5 24.3 %all-reduce.6.cloned.1.call-done = bf16[1024,1024]{1,0:T(8,128)(2,1)} async-done(((bf16[1024,1024]{1,0:T(8,128)(2,1)}), bf16[1024,1024]{1,0:T(8,128)(2,1)}) %all-reduce.6.cloned.1.call-update) | async-done | bytes 2097168 | tf_op jit(solution)/shard_map/psum | solution.py:185
  366.0 5.8 multiply_reduce_fusion
  387.3 51.5 %all-reduce.8.cloned.1.call-done = bf16[1024,1024]{1,0:T(8,128)(2,1)} async-done(((bf16[1024,1024]{1,0:T(8,128)(2,1)}), bf16[1024,1024]{1,0:T(8,128)(2,1)}) %all-reduce.8.cloned.1.call-update) | async-done | bytes 2097168 | tf_op jit(solution)/shard_map/psum | solution.py:202
  438.8 5.4 multiply_reduce_fusion.1
  455.9 7.8 multiply_reduce_fusion.7
  466.6 25.0 %while.29 = (s32[]{:T(128)}, f32[256,4,4,64]{0,3,2,1:T(8,128)}, bf16[2,512,4,512]{1,3,2,0:T(8,128)(2,1)}, bf16[2,512,4,4,64]{1,4,3,2,0:T(8,128)(2,1)S(1)}, bf16[...) while((s32[]{:T(128)}, f32[256,4,4,64]{0,3,2,1:T(8,128)}, ...), condition=%wide.region_21.22_spmd.clone, body=%wide.region_20.21_spmd.clone.sunk | while | flops 1364983808 | bytes 76595896 | solution.py:225
  487.4 4.3 fusion.160
  491.6 7.3 copy.94
  505.1 70.8 %reduce-scatter.8.cloned.1.call-done = bf16[256,4,512]{2,0,1:T(8,128)(2,1)} async-done(((bf16[1024,4,512]{2,0,1:T(8,128)(2,1)}), bf16[256,4,512]{2,0,1:T(8,128)(2,1)}) %reduce-scatter.8.cloned.1.call-update) | async-done | bytes 1048592 | tf_op jit(solution)/shard_map/reduce_scatter | solution.py:227
  581.9 5.5 add_convert_fusion
  587.5 52.0 %all-reduce.10.cloned.1.call-done = bf16[1024,1024]{1,0:T(8,128)(2,1)} async-done(((bf16[1024,1024]{1,0:T(8,128)(2,1)}), bf16[1024,1024]{1,0:T(8,128)(2,1)}) %all-reduce.10.cloned.1.call-update) | async-done | bytes 2097168 | tf_op jit(solution)/shard_map/psum | solution.py:241
  639.5 5.4 fusion.68
  644.9 5.2 reshape.219
  663.6 7.4 fusion.63
  671.2 6.6 fusion.79
  690.6 38.8 %all-reduce = (f32[]{:T(128)}, f32[1024]{0:T(1024)}, f32[256]{0:T(256)}, f32[256]{0:T(256)}, f32[1024]{0:T(1024)}, /*index=5*/f32[1024]{0:T(1024)}, f32[1024]{0:...) all-reduce(f32[]{:T(128)} %get-tuple-element.280, ...), channel_id=1, replica_groups=mesh['shard'=2,'ctx'=4,'tensor'=4] {'shard','ctx'}, use_global_device_ids=true, to_apply=%region_11.12 | all-reduce | flops 8705 | bytes 69640 | tf_op jit(solution)/shard_map/psum | solution.py:191
  735.5 64.8 %reduce-scatter.10.cloned.1.call-done = f32[128,256]{1,0:T(8,128)} async-done(((f32[1024,256]{1,0:T(8,128)}), f32[128,256]{1,0:T(8,128)}) %reduce-scatter.10.cloned.1.call-update) | async-done | bytes 131088 | tf_op jit(solution)/shard_map/reduce_scatter | solution.py:278
  800.3 66.4 %reduce-scatter.16.cloned.1.call-done = f32[128,256]{1,0:T(8,128)} async-done(((f32[1024,256]{1,0:T(8,128)}), f32[128,256]{1,0:T(8,128)}) %reduce-scatter.16.cloned.1.call-update) | async-done | bytes 131088 | tf_op jit(solution)/shard_map/reduce_scatter | solution.py:281
  866.7 91.6 %reduce-scatter.18.cloned.1.call-done = f32[128,1024]{1,0:T(8,128)} async-done(((f32[1024,1024]{1,0:T(8,128)}), f32[128,1024]{1,0:T(8,128)}) %reduce-scatter.18.cloned.1.call-update) | async-done | bytes 524304 | tf_op jit(solution)/shard_map/reduce_scatter | solution.py:282
  958.3 91.8 %reduce-scatter.20.cloned.1.call-done = f32[128,1024]{1,0:T(8,128)} async-done(((f32[1024,1024]{1,0:T(8,128)}), f32[128,1024]{1,0:T(8,128)}) %reduce-scatter.20.cloned.1.call-update) | async-done | bytes 524304 | tf_op jit(solution)/shard_map/reduce_scatter | solution.py:283
  1050.1 67.3 %reduce-scatter.14.cloned.1.call-done = f32[128,256]{1,0:T(8,128)} async-done(((f32[1024,256]{1,0:T(8,128)}), f32[128,256]{1,0:T(8,128)}) %reduce-scatter.14.cloned.1.call-update) | async-done | bytes 131088 | tf_op jit(solution)/shard_map/reduce_scatter | solution.py:280
  1117.4 66.4 %reduce-scatter.12.cloned.1.call-done = f32[128,256]{1,0:T(8,128)} async-done(((f32[1024,256]{1,0:T(8,128)}), f32[128,256]{1,0:T(8,128)}) %reduce-scatter.12.cloned.1.call-update) | async-done | bytes 131088 | tf_op jit(solution)/shard_map/reduce_scatter | solution.py:279
  (237 shorter events, 148.4 us)
Async XLA Ops:
  7.2 73.8 %all-gather.7.cloned.1.call-start = ((), (), s32[]{:S(2)}) async-start(), calls=%async_computation.7 | async-start | bytes 2621440 | tf_op jit(solution)/shard_map/all_gather | solution.py:160
  13.3 5.3 copy-start.29
  18.7 14.5 %copy-start.30 = (bf16[512,256]{1,0:T(8,128)(2,1)S(1)}, bf16[512,256]{1,0:T(8,128)(2,1)}, u32[]{:S(2)}) copy-start(bf16[512,256]{1,0:T(8,128)(2,1)} %param.34) | copy-start | bytes 786436
  28.7 12.6 %copy-start.16 = (bf16[1024,256]{1,0:T(8,128)(2,1)}, bf16[1024,256]{1,0:T(8,128)(2,1)S(1)}, u32[]{:S(2)}) copy-start(bf16[1024,256]{1,0:T(8,128)(2,1)S(1)} %all_gather.32) | copy-start | bytes 1572868
  28.7 13.4 %copy-start.44 = (f32[256]{0:T(256)S(1)}, f32[256]{0:T(256)}, u32[]{:S(2)}) copy-start(f32[256]{0:T(256)} %param.35) | copy-start | bytes 3076
  33.1 13.4 %copy-start.31 = (bf16[512,256]{1,0:T(8,128)(2,1)S(1)}, bf16[512,256]{1,0:T(8,128)(2,1)}, u32[]{:S(2)}) copy-start(bf16[512,256]{1,0:T(8,128)(2,1)} %param.31) | copy-start | bytes 786436
  33.1 94.5 %all-gather.9.cloned.1.call-start = ((), (), s32[]{:S(2)}) async-start(), calls=%async_computation.8 | async-start | bytes 2621440 | tf_op jit(solution)/shard_map/all_gather | solution.py:161
  42.1 11.8 copy-start.45
  46.4 186.8 %all-gather.15.cloned.1.call-start = ((), (), s32[]{:S(2)}) async-start(), calls=%async_computation.22 | async-start | bytes 10485760 | tf_op jit(solution)/shard_map/all_gather | solution.py:170
  53.9 4.4 copy-start.32
  140.1 5.8 copy-start.2
  154.2 5.8 copy-start.2
  176.6 91.2 %all-gather.11.cloned.1.call-start = ((), (), s32[]{:S(2)}) async-start(), calls=%async_computation.9 | async-start | bytes 3145728 | tf_op jit(solution)/shard_map/all_gather | solution.py:178
  177.1 125.2 %all-gather.13.cloned.1.call-start = ((), (), s32[]{:S(2)}) async-start(), calls=%async_computation.10 | async-start | bytes 3145728 | tf_op jit(solution)/shard_map/all_gather | solution.py:179
  177.7 182.1 %all-reduce.6.cloned.1.call-start = ((), (), s32[]{:S(2)}) async-start(), calls=%async_computation.11 | async-start | bytes 4194304 | tf_op jit(solution)/shard_map/psum | solution.py:185
  240.6 5.4 copy-start.34
  251.2 4.6 copy-start.4
  251.2 4.7 copy-start.12
  255.9 11.9 copy-start.33
  255.9 11.9 copy-start.43
  255.9 11.9 copy-start.48
  302.3 6.0 copy-start.39
  308.2 51.6 %copy-start.41 = (f32[1024]{0:T(1024)S(1)}, f32[1024]{0:T(1024)}, u32[]{:S(2)}) copy-start(f32[1024]{0:T(1024)} %param.43) | copy-start | bytes 12292
  308.3 130.6 %all-reduce.8.cloned.1.call-start = ((), (), s32[]{:S(2)}) async-start(), calls=%async_computation.12 | async-start | bytes 4194304 | tf_op jit(solution)/shard_map/psum | solution.py:202
  371.7 5.1 copy-start.51
  373.7 4.8 copy-start.50
  376.9 5.3 copy-start.24
  378.5 5.0 copy-start.46
  387.2 188.7 %reduce-scatter.8.cloned.1.call-start = ((), (), s32[]{:S(2)}) async-start(), calls=%async_computation.13 | async-start | bytes 5242880 | tf_op jit(solution)/shard_map/reduce_scatter | solution.py:227
  438.8 5.4 copy-start.6
  438.8 6.5 copy-start.8
  438.8 7.1 copy-start.15
  498.9 140.6 %all-reduce.10.cloned.1.call-start = ((), (), s32[]{:S(2)}) async-start(), calls=%async_computation.14 | async-start | bytes 4194304 | tf_op jit(solution)/shard_map/psum | solution.py:241
  502.4 75.3 %copy-start.17 = (bf16[1024,256]{1,0:T(8,128)(2,1)S(1)}, bf16[1024,256]{1,0:T(8,128)(2,1)}, u32[]{:S(2)}) copy-start(bf16[1024,256]{1,0:T(8,128)(2,1)} %copy-done.16) | copy-start | bytes 1572868
  575.9 4.4 copy-start.28
  587.4 145.5 %all-reduce.12.cloned.1.call-start = ((), (), s32[]{:S(2)}) async-start(), calls=%async_computation.15 | async-start | bytes 2097152 | tf_op jit(solution)/shard_map/psum | solution.py:261
  650.0 4.7 copy-start.11
  654.6 145.7 %reduce-scatter.10.cloned.1.call-start = ((), (), s32[]{:S(2)}) async-start(), calls=%async_computation.16 | async-start | bytes 1179648 | tf_op jit(solution)/shard_map/reduce_scatter | solution.py:278
  660.1 206.5 %reduce-scatter.16.cloned.1.call-start = ((), (), s32[]{:S(2)}) async-start(), calls=%async_computation.19 | async-start | bytes 1179648 | tf_op jit(solution)/shard_map/reduce_scatter | solution.py:281
  663.5 294.8 %reduce-scatter.18.cloned.1.call-start = ((), (), s32[]{:S(2)}) async-start(), calls=%async_computation.20 | async-start | bytes 4718592 | tf_op jit(solution)/shard_map/reduce_scatter | solution.py:282
  671.0 379.1 %reduce-scatter.20.cloned.1.call-start = ((), (), s32[]{:S(2)}) async-start(), calls=%async_computation.21 | async-start | bytes 4718592 | tf_op jit(solution)/shard_map/reduce_scatter | solution.py:283
  677.8 439.5 %reduce-scatter.14.cloned.1.call-start = ((), (), s32[]{:S(2)}) async-start(), calls=%async_computation.18 | async-start | bytes 1179648 | tf_op jit(solution)/shard_map/reduce_scatter | solution.py:280
  683.9 4.4 copy-start.14
  683.9 6.6 copy-start.36
  684.0 6.6 copy-start.37
  684.0 6.6 copy-start.38
  684.0 499.8 %reduce-scatter.12.cloned.1.call-start = ((), (), s32[]{:S(2)}) async-start(), calls=%async_computation.17 | async-start | bytes 1179648 | tf_op jit(solution)/shard_map/reduce_scatter | solution.py:279
  684.0 499.7 %copy-start.1 = (bf16[256,1024]{1,0:T(8,128)(2,1)S(1)}, bf16[256,1024]{1,0:T(8,128)(2,1)}, u32[]{:S(2)}) copy-start(bf16[256,1024]{1,0:T(8,128)(2,1)} %param.29) | copy-start | bytes 1572868
  (23 other events, 53.3 us)
Sparse Core Ops, SparseCore 0:
  33.2 47.7 all-gather.6
  83.1 44.4 all-gather.8
  176.7 56.5 all-gather.14
  234.6 33.1 all-gather.10
  269.2 33.1 all-gather.12
  308.4 51.3 all-reduce.5
  387.3 51.4 all-reduce.7
  499.1 76.8 reduce-scatter.7
  587.6 51.8 all-reduce.9
  654.8 78.1 all-reduce.11
  737.3 62.8 reduce-scatter.9
  804.1 62.5 reduce-scatter.15
  871.3 86.9 reduce-scatter.17
  962.4 87.6 reduce-scatter.19
  1054.3 63.0 reduce-scatter.13
  1121.2 62.5 reduce-scatter.11
